TPU v7x, 32 devices: a whole 2x2x4 slice. The times are simulated.
32 devices in a mesh: mp: 8 (over z, y), dp: 4 (over x, core).
Axes of the slice: x: 2, y: 2, z: 4, core: 2. Of those that a mesh axis runs over, the one named last changes fastest.
Arguments:
- forward_fields: bfloat16 [16, 4, 16384], P(None, None, 'mp'), may hold values from -6 to 6
- adjoint_fields: bfloat16 [64, 4, 16384], P(None, None, 'mp'), may hold values from -6 to 6
- data_rec: int32 [768], P('dp'), may hold values from 0 to 63
- data_freq: int32 [768], P('dp'), may hold values from 0 to 15
- data_coef: float32 [768, 4], P('dp'), may hold values from -6 to 6
- residual_cols: bfloat16 [768, 256], P('dp'), may hold values from -6 to 6
Outputs:
- data_update: bfloat16 [768, 256], P('dp')
- model_update: float32 [16384, 256], P(('mp', 'dp'))
All inputs are finite; a program needn't handle non-finite values.
Results may differ from a plain program's by a relative error of at most 0.0075.
Values may be sent and summed in bfloat16 or wider, within the bound.
A program may use at most 64 MiB of HBM per device.

v0:
```python
import math

import jax
import jax.numpy as jnp
from jax import lax
from jax.sharding import PartitionSpec as P

GRID_COLS = 128
SWEEPS = 2


def with_halo(array, sides, width):
    for axis, dim in sides:
        peers, length = (lax.axis_size(axis), array.shape[dim])
        up = [(i, (i + 1) % peers) for i in range(peers - 1)]
        down = [(j, i) for i, j in up]
        last = lax.slice_in_dim(array, length - width, length, axis=dim)
        leading = lax.slice_in_dim(array, 0, width, axis=dim)
        before = lax.ppermute(last, axis, up)
        after = lax.ppermute(leading, axis, down)
        array = jnp.concatenate([before, array, after], axis=dim)
    return array


def sweep_once(field):
    center = field[:, 1:-1, :]
    sides = jnp.pad(center, ((0, 0), (0, 0), (1, 1)))
    beside_all = field[:, :-2, :] + field[:, 2:, :] + sides[:, :, :-2] + sides[:, :, 2:]
    return center + 0.2 * (beside_all - 4.0 * center)


def per_device(forward_fields, adjoint_fields, data_rec, data_freq, data_coef, residual_cols):
    rows_here = data_rec.shape[0]
    cells_here = forward_fields.shape[2]
    slab_rows = cells_here // GRID_COLS
    slab_count = lax.axis_size("mp")
    block_count = lax.axis_size("dp")
    adjoint = adjoint_fields[data_rec].astype(jnp.float32)
    forward = forward_fields[data_freq].astype(jnp.float32)
    sens = (0.5 * jnp.sum(data_coef[:, :, None] * adjoint * forward, axis=1)).astype(jnp.bfloat16)
    grid = sens.astype(jnp.float32).reshape(rows_here, slab_rows, GRID_COLS)
    extended = with_halo(grid.astype(jnp.bfloat16), (("mp", 1),), SWEEPS).astype(grid.dtype)
    first_row = lax.axis_index("mp") * slab_rows
    total_rows = slab_rows * slab_count
    for sweep in range(SWEEPS):
        extended = sweep_once(extended)
        margin = SWEEPS - 1 - sweep
        if margin > 0:
            global_rows = first_row - margin + jnp.arange(slab_rows + 2 * margin, dtype=jnp.int32)
            inside = (global_rows >= 0) & (global_rows < total_rows)
            extended = jnp.where(inside[None, :, None], extended, 0.0)
    grid = extended
    smooth = grid.reshape(rows_here, cells_here).astype(jnp.bfloat16)
    residual_whole = lax.all_gather(residual_cols, "dp", axis=0, tiled=True)
    gram_tile = lax.dot_general(
        smooth,
        lax.all_gather(sens, "dp", axis=0, tiled=True),
        (((1,), (1,)), ((), ())),
        preferred_element_type=jnp.float32,
    )
    partial_value = jnp.dot(
        gram_tile, residual_whole.astype(jnp.float32), precision=lax.Precision.HIGHEST
    )
    gram_prod = lax.psum(partial_value, "mp") / (cells_here * slab_count)
    data_update = (gram_prod + residual_cols.astype(jnp.float32)).astype(jnp.bfloat16)
    summed = lax.psum_scatter(
        lax.dot_general(
            smooth, data_update, (((0,), (0,)), ((), ())), preferred_element_type=jnp.float32
        ),
        "dp",
        scatter_dimension=0,
        tiled=True,
    )
    model_update = summed / math.sqrt(rows_here * block_count)
    return (data_update, model_update)


def solution(mesh):
    in_specs = (
        P(None, None, "mp"),
        P(None, None, "mp"),
        P("dp"),
        P("dp"),
        P("dp", None),
        P("dp", None),
    )
    out_specs = (P("dp", None), P(("mp", "dp"), None))
    return jax.shard_map(
        per_device, mesh=mesh, in_specs=in_specs, out_specs=out_specs, check_vma=False
    )
```

profile of v0, /device:TPU:0, one launch (start us, length us, event | category | flops | bytes accessed | tf_op | source)
XLA Modules:
  0.0 189.3 jit_solution(5085543405692865950)
XLA Ops:
  7.2 0.0 copy-start
  7.2 0.0 all-gather.2.cloned.1.call-start
  7.2 0.8 compare_select_fusion.1
  8.0 0.7 compare_select_fusion
  8.7 0.8 copy.10
  9.5 0.0 copy-done
  9.5 0.0 copy-start.1
  9.5 9.6 %gather_fusion = bf16[192,4,2048]{2,1,0:T(4,128)(2,1)} fusion(bf16[64,4,2048]{2,1,0:T(4,128)(2,1)S(1)} %copy-done, s32[1024]{0:T(1024)S(1)} %pad_clamp_fusion.1), kind=kCustom, calls=%fused_computation | custom fusion | bytes 6292224 | tf_op jit(solution)/shard_map/gather | solution.py:38
  19.1 0.0 copy-done.1
  19.1 9.7 %gather_fusion.1 = bf16[192,4,2048]{2,1,0:T(4,128)(2,1)} fusion(bf16[16,4,2048]{2,1,0:T(4,128)(2,1)S(1)} %copy-done.1, s32[1024]{0:T(1024)S(1)} %pad_clamp_fusion), kind=kCustom, calls=%fused_computation.1 | custom fusion | bytes 6292224 | tf_op jit(solution)/shard_map/gather | solution.py:39
  28.8 9.7 %multiply_reduce_fusion = f32[192,2048]{1,0:T(8,128)S(1)} fusion(bf16[192,4,2048]{2,1,0:T(4,128)(2,1)} %gather_fusion.1, bf16[192,4,2048]{2,1,0:T(4,128)(2,1)} %gather_fusion, f32[192,4]{1,0:T(8,128)S(1)} %copy.10), kind=kLoop, calls=%fused_computation.2 | loop fusion | flops 7471104 | bytes 7867392 | tf_op jit(solution)/shard_map/reduce_sum | solution.py:40
  38.5 0.0 copy-start.3
  38.5 1.0 multiply_convert_fusion
  39.5 0.0 all-gather.2.cloned.1.call-update
  39.5 0.0 all-reduce.4.cloned.1.call-start
  39.6 1.4 copy.14
  41.0 4.9 %collective-permute-start = (bf16[192,2,128]{0,2,1:T(8,128)(2,1)S(1)}, bf16[192,2,128]{0,2,1:T(8,128)(2,1)S(1)}, u32[]{:S(2)}, u32[]{:S(2)}) collective-permute-start(bf16[192,2,128]{0,2,1:T(8,128)(2,1)S(1)} %get-tuple-element.2), channel_id=1, source_target_pairs={{0,4},{4,8},{8,12},{12,16},{16,20},{20,24},{24,28},{1,5},{5,9},{9,... | collective-permute-start | bytes 294920 | tf_op jit(solution)/shard_map/ppermute | solution.py:19
  45.9 1.3 collective-permute-start.1
  47.3 0.0 copy-done.3
  47.3 7.1 %all_gather.7 = bf16[768,256]{1,0:T(8,128)(2,1)S(1)} all-gather(bf16[192,256]{1,0:T(8,128)(2,1)S(1)} %copy-done.3), channel_id=1, replica_groups=mesh['mp'=8,'dp'=4] {'dp'}, dimensions={0}, use_global_device_ids=true | all-gather | bytes 491520 | tf_op jit(solution)/shard_map/all_gather | solution.py:54
  54.4 0.0 collective-permute-done
  54.4 0.0 collective-permute-done.1
  54.4 0.3 maximum_convert_fusion
  54.7 0.2 slice.54
  55.0 1.0 fusion.5
  55.9 0.1 slice.57
  56.1 0.8 fusion.11
  56.9 14.4 %all-gather.2.cloned.1.call-done = bf16[768,2048]{1,0:T(8,128)(2,1)} async-done(((bf16[192,2048]{1,0:T(8,128)(2,1)}), bf16[768,2048]{1,0:T(8,128)(2,1)}) %all-gather.2.cloned.1.call-update) | async-done | bytes 3145744 | tf_op jit(solution)/shard_map/all_gather | solution.py:57
  71.3 3.1 %fusion.13 = f32[192,768]{1,0:T(8,128)S(1)} fusion(bf16[192,2048]{0,1:T(8,128)(2,1)S(1)} %bitcast.10, bf16[768,2048]{1,0:T(8,128)(2,1)} %all-gather.2.cloned.1.call-done), kind=kOutput, calls=%fused_computation.31 | convolution fusion | flops 603979776 | bytes 4521984 | tf_op jit(solution)/shard_map/dot_general | solution.py:55
  74.4 1.1 fusion.14
  75.5 0.0 all-reduce.4.cloned.1.call-update
  75.5 0.0 reduce-scatter.2.cloned.1.call-start
  75.6 72.2 %all-reduce.4.cloned.1.call-done = f32[192,256]{1,0:T(8,128)} async-done(((f32[192,256]{1,0:T(8,128)}), f32[192,256]{1,0:T(8,128)}) %all-reduce.4.cloned.1.call-update) | async-done | bytes 196624 | tf_op jit(solution)/shard_map/psum | solution.py:64
  147.8 1.0 add_convert_fusion
  148.7 0.0 copy-start.2
  148.7 1.8 fusion.15
  150.5 0.0 reduce-scatter.2.cloned.1.call-update
  150.5 0.0 copy-done.2
  150.5 30.3 %reduce-scatter.2.cloned.1.call-done = f32[512,256]{1,0:T(8,128)} async-done(((f32[2048,256]{1,0:T(8,128)}), f32[512,256]{1,0:T(8,128)}) %reduce-scatter.2.cloned.1.call-update) | async-done | bytes 524304 | tf_op jit(solution)/shard_map/reduce_scatter | solution.py:66
  180.9 1.9 broadcast_multiply_fusion
  (4 shorter events, 0.0 us)
Async XLA Ops:
  7.2 2.3 %copy-start = (bf16[64,4,2048]{2,1,0:T(4,128)(2,1)S(1)}, bf16[64,4,2048]{2,1,0:T(4,128)(2,1)}, u32[]{:S(2)}) copy-start(bf16[64,4,2048]{2,1,0:T(4,128)(2,1)} %param.7) | copy-start | bytes 3145732
  7.2 64.1 %all-gather.2.cloned.1.call-start = ((), (), s32[]{:S(2)}) async-start(), calls=%async_computation.1 | async-start | bytes 3932160 | tf_op jit(solution)/shard_map/all_gather | solution.py:57
  9.5 9.6 %copy-start.1 = (bf16[16,4,2048]{2,1,0:T(4,128)(2,1)S(1)}, bf16[16,4,2048]{2,1,0:T(4,128)(2,1)}, u32[]{:S(2)}) copy-start(bf16[16,4,2048]{2,1,0:T(4,128)(2,1)} %param.6) | copy-start | bytes 786436
  38.5 8.8 %copy-start.3 = (bf16[192,256]{1,0:T(8,128)(2,1)S(1)}, bf16[192,256]{1,0:T(8,128)(2,1)}, u32[]{:S(2)}) copy-start(bf16[192,256]{1,0:T(8,128)(2,1)} %param.11) | copy-start | bytes 294916
  39.5 108.3 %all-reduce.4.cloned.1.call-start = ((), (), s32[]{:S(2)}) async-start(), calls=%async_computation.2 | async-start | bytes 393216 | tf_op jit(solution)/shard_map/psum | solution.py:64
  41.0 13.4 %collective-permute-start = (bf16[192,2,128]{0,2,1:T(8,128)(2,1)S(1)}, bf16[192,2,128]{0,2,1:T(8,128)(2,1)S(1)}, u32[]{:S(2)}, u32[]{:S(2)}) collective-permute-start(bf16[192,2,128]{0,2,1:T(8,128)(2,1)S(1)} %get-tuple-element.2), channel_id=1, source_target_pairs={{0,4},{4,8},{8,12},{12,16},{16,20},{20,24},{24,28},{1,5},{5,9},{9,... | collective-permute-start | bytes 294920 | tf_op jit(solution)/shard_map/ppermute | solution.py:19
  45.9 8.4 %collective-permute-start.1 = (bf16[192,2,128]{0,2,1:T(8,128)(2,1)S(1)}, bf16[192,2,128]{0,2,1:T(8,128)(2,1)S(1)}, u32[]{:S(2)}, u32[]{:S(2)}) collective-permute-start(bf16[192,2,128]{0,2,1:T(8,128)(2,1)S(1)} %get-tuple-element.3), channel_id=1, source_target_pairs={{4,0},{8,4},{12,8},{16,12},{20,16},{24,20},{28,24},{5,1},{9,5},{13... | collective-permute-start | bytes 294920 | tf_op jit(solution)/shard_map/ppermute | solution.py:20
  75.5 105.4 %reduce-scatter.2.cloned.1.call-start = ((), (), s32[]{:S(2)}) async-start(), calls=%async_computation.3 | async-start | bytes 2621440 | tf_op jit(solution)/shard_map/reduce_scatter | solution.py:66
  148.7 1.8 copy-start.2
Sparse Core Ops, SparseCore 0:
  39.6 31.6 all-gather.1
  75.7 72.0 all-reduce.3
  150.7 30.1 reduce-scatter.1
where the time goes:
time: 190 us; the launch traced here: 189 us
  waiting for transfers between devices  117 us (62%)
  local copies, waits for them, and re-layouts  21.9 us (12%)
  other arithmetic  17.1 us (9%)
  between operations  13.9 us (7%)
  blocking collectives  7.12 us (4%)
  starting transfers between devices  6.32 us (3%)
  matrix products  5.99 us (3%)
    psum x1, waiting for transfers between devices, per_device(): gram_prod = lax.psum(partial_value, 'mp') / (cells_here * slab_count)  72.2 us
    reduce_scatter x1, waiting for transfers between devices, per_device(): lax.psum_scatter(lax.dot_general(smooth, data_update, (((0,), (0,)), ((),...  30.3 us
    all_gather x1, waiting for transfers between devices, per_device(): lax.all_gather(sens, 'dp', axis=0, tiled=True)  14.4 us
    gather x1, local copies, waits for them, and re-layouts, per_device(): forward = forward_fields[data_freq].astype(jnp.float32)  9.69 us
    reduce_sum x1, other arithmetic, per_device(): jnp.sum(data_coef[:, :, None] * adjoint * forward, axis=1)  9.66 us
    gather x1, local copies, waits for them, and re-layouts, per_device(): adjoint = adjoint_fields[data_rec].astype(jnp.float32)  9.62 us
    all_gather x1, blocking collectives, per_device(): residual_whole = lax.all_gather(residual_cols, 'dp', axis=0, tiled=True)  7.12 us
    ppermute x1, starting transfers between devices, with_halo(): before = lax.ppermute(last, axis, up)  4.91 us
  transfers between devices with their start and end apart: 5, of which 3 were waited for; matrix products, arithmetic and copies ran while one was open for 2% of the time, Pallas kernels for 0%

commit v1 on v0

v1 whole, which is shorter than its diff:
```python
import functools
import math

import jax
import jax.numpy as jnp
from jax import lax
from jax.experimental import pallas as pl
from jax.experimental.pallas import tpu as pltpu
from jax.sharding import PartitionSpec as P

COLS = 128
HALO = 2
MESH = pl.DeviceIdType.MESH
F32, BF16 = jnp.float32, jnp.bfloat16


def plan(rows_here, n_mp):
    chunk = 16 * -(-rows_here // (16 * n_mp))
    chunks = rows_here // chunk
    return chunk, chunks, (n_mp - chunks) // 2


def remote(src, dst, send, recv, axis, index):
    return pltpu.make_async_remote_copy(
        src_ref=src, dst_ref=dst, send_sem=send, recv_sem=recv,
        device_id={axis: index}, device_id_type=MESH,
    )


def kernel(
    n_mp, n_dp, ka, kf,
    meta_ref, r_ref, af_ref, du_ref, model_ref,
    meta_all, r_all, win, ohr, ohf, sens, smat, smooth, smooth_t, psend, precv, q, q2, du_all,
    local_sem, halo_send, halo_recv, meta_send, meta_recv, r_send, r_recv,
    s1_send, s1_recv, s2_send, s2_recv, g_send, g_recv, d_send, d_recv,
):
    d, m = lax.axis_index("dp"), lax.axis_index("mp")
    rows_here, rhs = r_ref.shape
    slab = af_ref.shape[1] // COLS
    own = slab // n_dp
    window = own + 2 * HALO
    comps = ohr.shape[0]
    chunk, chunks, first = plan(rows_here, n_mp)
    total_cells = slab * n_mp * COLS

    def dp_peer(t):
        return lax.rem(d + t, n_dp)

    def mp_peer(t):
        return lax.rem(m + t, n_mp)

    def block(index):
        return pl.ds(pl.multiple_of(index * rows_here, 16), rows_here)

    def chunk_of(index, c):
        return pl.ds(pl.multiple_of(index * rows_here + c * chunk, 16), chunk)

    def grid_row(index):
        return pl.ds(pl.multiple_of(index * COLS, COLS), COLS)

    barrier = pltpu.get_barrier_semaphore()
    for t in range(1, n_dp):
        pl.semaphore_signal(barrier, inc=1, device_id={"dp": dp_peer(t)}, device_id_type=MESH)
    for t in range(1, n_mp):
        pl.semaphore_signal(barrier, inc=1, device_id={"mp": mp_peer(t)}, device_id_type=MESH)

    def slab_row(w):
        return d * own - HALO + w

    def in_slab(w):
        return (slab_row(w) >= 0) & (slab_row(w) < slab)

    def local_copy(w):
        return pltpu.make_async_copy(
            af_ref.at[:, grid_row(jnp.clip(slab_row(w), 0, slab - 1))],
            win.at[:, w * COLS:(w + 1) * COLS],
            local_sem.at[w],
        )

    for w in range(window):
        pl.when(in_slab(w))(local_copy(w).start)
    edges = [w for w in range(window) if w < HALO or w >= own + HALO]

    def halo_copy(w):
        step = 1 if w < HALO else -1
        return remote(
            af_ref.at[:, grid_row(jnp.clip(slab_row(w) + step * slab, 0, slab - 1))],
            win.at[:, w * COLS:(w + 1) * COLS],
            halo_send.at[w], halo_recv.at[w], "mp", jnp.clip(m + step, 0, n_mp - 1),
        )

    def halo_sends(w):
        return (slab_row(w) < 0) & (m < n_mp - 1) if w < HALO else (slab_row(w) >= slab) & (m > 0)

    def halo_arrives(w):
        return (slab_row(w) < 0) & (m > 0) if w < HALO else (slab_row(w) >= slab) & (m < n_mp - 1)

    def beyond_grid(w):
        return (slab_row(w) < 0) & (m == 0) if w < HALO else (slab_row(w) >= slab) & (m == n_mp - 1)

    def meta_copy(t):
        return remote(meta_ref, meta_all.at[d], meta_send.at[t], meta_recv.at[d], "dp", dp_peer(t))

    def r_copy(t):
        return remote(r_ref, r_all.at[block(d)], r_send.at[t], r_recv.at[d], "dp", dp_peer(t))

    pl.semaphore_wait(barrier, n_dp + n_mp - 2)
    for t in range(1, n_dp):
        meta_copy(t).start()
    for w in edges:
        pl.when(halo_sends(w))(halo_copy(w).start)
    for t in range(1, n_dp):
        r_copy(t).start()

    meta_all[d] = meta_ref[...]
    r_all[block(d)] = r_ref[...]

    def clear(w):
        win[:, w * COLS:(w + 1) * COLS] = jnp.zeros((ka + 2 * kf, COLS), BF16)

    for w in edges:
        pl.when(beyond_grid(w))(functools.partial(clear, w))

    at = lax.broadcasted_iota(jnp.int32, (COLS, COLS), 0)
    to = lax.broadcasted_iota(jnp.int32, (COLS, COLS), 1)
    apart = jnp.abs(at - to)
    ends = jnp.where(to == 0, 1.0, 0.0) + jnp.where(to == COLS - 1, 1.0, 0.0)
    eye = jnp.where(apart == 0, 1.0, 0.0)
    bands = (
        eye * (5.0 - ends) + jnp.where(apart == 1, 2.0, 0.0) + jnp.where(apart == 2, 1.0, 0.0),
        jnp.where(apart <= 1, 2.0, 0.0),
        eye,
    )
    last_row = slab * n_mp - 1
    for o in range(own):
        row = m * slab + d * own + o
        missing = jnp.where(row == 0, 1.0, 0.0) + jnp.where(row == last_row, 1.0, 0.0)
        for w in range(window):
            gap = abs(w - o - HALO)
            if gap > 2:
                value = jnp.zeros((COLS, COLS), F32)
            else:
                value = bands[gap] - missing * eye if gap == 0 else bands[gap]
            smat[w * COLS:(w + 1) * COLS, o * COLS:(o + 1) * COLS] = value.astype(BF16)

    for t in range(1, n_dp):
        source = dp_peer(t)
        remote(meta_ref, meta_all.at[source], meta_send.at[t], meta_recv.at[source], "dp", source).wait_recv()
    for j in range(n_dp):
        cols = jnp.transpose(meta_all[j])[:rows_here]
        here = slice(j * rows_here, (j + 1) * rows_here)
        ia = lax.broadcasted_iota(jnp.int32, (rows_here, ka), 1).astype(F32)
        jf = lax.broadcasted_iota(jnp.int32, (rows_here, kf), 1).astype(F32)
        for k in range(comps):
            ohr[k, here] = jnp.where(ia == cols[:, 0:1] + float(k), 1.0, 0.0).astype(BF16)
            weight = jnp.where(jf == cols[:, 1:2] + float(k), cols[:, 2 + k:3 + k], 0.0)
            high = weight.astype(BF16)
            ohf[k, here, :kf] = high
            ohf[k, here, kf:] = (weight - high.astype(F32)).astype(BF16)

    wide = 2 if window % 2 == 0 else 1
    tiles = sorted(range(window // wide), key=lambda i: i * wide in edges or i * wide + wide - 1 in edges)
    for i in tiles:
        for w in range(i * wide, (i + 1) * wide):
            pl.when(in_slab(w))(local_copy(w).wait)
            if w in edges:
                pl.when(halo_arrives(w))(halo_copy(w).wait_recv)
        lanes = slice(i * wide * COLS, (i + 1) * wide * COLS)
        for j in range(n_dp):
            here = slice(j * rows_here, (j + 1) * rows_here)
            value = None
            for k in range(comps):
                adjoint = jnp.dot(ohr[k, here], win[:ka, lanes], preferred_element_type=F32)
                forward = jnp.dot(ohf[k, here], win[ka:, lanes], preferred_element_type=F32)
                value = adjoint * forward if value is None else value + adjoint * forward
            sens[here, lanes] = value.astype(BF16)
    smooth[...] = (jnp.dot(sens[...], smat[...], preferred_element_type=F32) * 0.04).astype(BF16)

    for t in range(1, n_dp):
        source = dp_peer(t)
        remote(r_ref, r_all.at[block(source)], r_send.at[t], r_recv.at[source], "dp", source).wait_recv()
    back = lax.dot_general(
        sens[:, HALO * COLS:(HALO + own) * COLS], r_all[...],
        (((0,), (0,)), ((), ())), preferred_element_type=F32,
    ).astype(BF16)

    def p_copy(t):
        return remote(psend.at[t - 1], precv.at[d], s1_send.at[t], s1_recv.at[d], "dp", dp_peer(t))

    for t in range(1, n_dp):
        psend[t - 1] = jnp.dot(smooth[block(dp_peer(t))], back, preferred_element_type=F32).astype(BF16)
        p_copy(t).start()
    total = jnp.dot(smooth[block(d)], back, preferred_element_type=F32)
    smooth_t[...] = jnp.transpose(smooth[...])
    for t in range(1, n_dp):
        source = dp_peer(t)
        remote(psend.at[t - 1], precv.at[source], s1_send.at[t], s1_recv.at[source], "dp", source).wait_recv()
        total = total + precv[source].astype(F32)
    q[...] = total.astype(BF16)

    def q_copy(c):
        return remote(q.at[c * chunk:(c + 1) * chunk], q2.at[m], s2_send.at[c], s2_recv.at[m], "mp", first + c)

    for c in range(chunks):
        pl.when(m != first + c)(q_copy(c).start)
    mine = m - first
    owner = (mine >= 0) & (mine < chunks)
    mine = jnp.clip(mine, 0, chunks - 1)

    def g_copy(t):
        rows = chunk_of(d, mine)
        return remote(du_all.at[rows], du_all.at[rows], g_send.at[t], g_recv.at[mine], "mp", mp_peer(t))

    @pl.when(owner)
    def _():
        q2[m] = q[pl.ds(pl.multiple_of(mine * chunk, 16), chunk)]
        for t in range(1, n_mp):
            source = mp_peer(t)
            remote(q.at[:chunk], q2.at[source], s2_send.at[0], s2_recv.at[source], "mp", source).wait_recv()
        gram = q2[0].astype(F32)
        for i in range(1, n_mp):
            gram = gram + q2[i].astype(F32)
        residual = r_ref[pl.ds(pl.multiple_of(mine * chunk, 16), chunk)].astype(F32)
        du_all[chunk_of(d, mine)] = (gram * (1.0 / total_cells) + residual).astype(BF16)
        for t in range(1, n_mp):
            g_copy(t).start()

    def d_copy(t, c):
        rows = chunk_of(d, c)
        return remote(du_all.at[rows], du_all.at[rows], d_send.at[t, c], d_recv.at[d, c], "dp", dp_peer(t))

    for c in range(chunks):
        rows = chunk_of(d, c)
        arrived = remote(du_all.at[rows], du_all.at[rows], g_send.at[0], g_recv.at[c], "mp", first + c)
        pl.when(m != first + c)(arrived.wait_recv)
        for t in range(1, n_dp):
            d_copy(t, c).start()
    du_ref[...] = du_all[block(d)]
    for t in range(1, n_dp):
        source = dp_peer(t)
        for c in range(chunks):
            rows = chunk_of(source, c)
            remote(du_all.at[rows], du_all.at[rows], d_send.at[t, c], d_recv.at[source, c], "dp", source).wait_recv()
    model_ref[...] = jnp.dot(smooth_t[...], du_all[...], preferred_element_type=F32) * (
        1.0 / math.sqrt(rows_here * n_dp)
    )

    for w in edges:
        pl.when(halo_sends(w))(halo_copy(w).wait_send)
    for t in range(1, n_dp):
        meta_copy(t).wait_send()
        r_copy(t).wait_send()
        p_copy(t).wait_send()
        for c in range(chunks):
            d_copy(t, c).wait_send()
    for c in range(chunks):
        pl.when(m != first + c)(q_copy(c).wait_send)

    @pl.when(owner)
    def _():
        for t in range(1, n_mp):
            g_copy(t).wait_send()


def per_device(n_mp, n_dp, forward_fields, adjoint_fields, data_rec, data_freq, data_coef, residual_cols):
    rows_here, rhs = residual_cols.shape
    cells = forward_fields.shape[2]
    comps = forward_fields.shape[1]
    ka, kf = adjoint_fields.shape[0] * comps, forward_fields.shape[0] * comps
    data = rows_here * n_dp
    own = cells // COLS // n_dp
    window = own + 2 * HALO
    chunk, chunks, first = plan(rows_here, n_mp)
    forward = forward_fields.reshape(kf, cells)
    af = jnp.concatenate([adjoint_fields.reshape(ka, cells), forward, forward], axis=0)
    meta = jnp.concatenate(
        [(data_rec * comps)[None].astype(F32), (data_freq * comps)[None].astype(F32), 0.5 * data_coef.T],
        axis=0,
    )
    meta = jnp.pad(meta, ((0, 8 - meta.shape[0]), (0, -rows_here % 128)))
    dma = pltpu.SemaphoreType.DMA
    vmem = pl.BlockSpec(memory_space=pltpu.VMEM)
    return pl.pallas_call(
        functools.partial(kernel, n_mp, n_dp, ka, kf),
        out_shape=(
            jax.ShapeDtypeStruct((rows_here, rhs), BF16),
            jax.ShapeDtypeStruct((own * COLS, rhs), F32),
        ),
        in_specs=[vmem, vmem, pl.BlockSpec(memory_space=pl.ANY)],
        out_specs=(vmem, vmem),
        scratch_shapes=[
            pltpu.VMEM((n_dp,) + meta.shape, F32),
            pltpu.VMEM((data, rhs), BF16),
            pltpu.VMEM((ka + 2 * kf, window * COLS), BF16),
            pltpu.VMEM((comps, data, ka), BF16),
            pltpu.VMEM((comps, data, 2 * kf), BF16),
            pltpu.VMEM((data, window * COLS), BF16),
            pltpu.VMEM((window * COLS, own * COLS), BF16),
            pltpu.VMEM((data, own * COLS), BF16),
            pltpu.VMEM((own * COLS, data), BF16),
            pltpu.VMEM((n_dp - 1, rows_here, rhs), BF16),
            pltpu.VMEM((n_dp, rows_here, rhs), BF16),
            pltpu.VMEM((rows_here, rhs), BF16),
            pltpu.VMEM((n_mp, chunk, rhs), BF16),
            pltpu.VMEM((data, rhs), BF16),
            dma((window,)), dma((window,)), dma((window,)),
            dma((n_dp,)), dma((n_dp,)), dma((n_dp,)), dma((n_dp,)),
            dma((n_dp,)), dma((n_dp,)),
            dma((chunks,)), dma((n_mp,)),
            dma((n_mp,)), dma((chunks,)),
            dma((n_dp, chunks)), dma((n_dp, chunks)),
        ],
        compiler_params=pltpu.CompilerParams(collective_id=0, has_side_effects=True, vmem_limit_bytes=60 * 1024 * 1024),
    )(meta, residual_cols, af)


def solution(mesh):
    in_specs = (
        P(None, None, "mp"),
        P(None, None, "mp"),
        P("dp"),
        P("dp"),
        P("dp", None),
        P("dp", None),
    )
    out_specs = (P("dp", None), P(("mp", "dp"), None))
    body = functools.partial(per_device, mesh.shape["mp"], mesh.shape["dp"])
    return jax.shard_map(body, mesh=mesh, in_specs=in_specs, out_specs=out_specs, check_vma=False)
```

time: 190 us -> 46.2 us (0.24)
  waiting for transfers between devices: 117 us -> 0 us
  Pallas kernels: 0 us -> 38.4 us
  local copies, waits for them, and re-layouts: 21.9 us -> 4.87 us
  other arithmetic: 17.1 us -> 1.95 us
  between operations: 13.9 us -> 0.71 us
  blocking collectives: 7.12 us -> 0 us
  starting transfers between devices: 6.32 us -> 0 us
  matrix products: 5.99 us -> 0 us
    psum x1 -> x0, waiting for transfers between devices: 72.2 us -> none  [per_device(): gram_prod = lax.psum(partial_value, 'mp') / (cells_here * slab_count)]
    pallas_call x0 -> x1, Pallas kernels: none -> 38.4 us  [per_device(): pl.pallas_call(functools.partial(kernel, n_mp, n_dp, ka, kf), out_shape=(...]
    reduce_scatter x1 -> x0, waiting for transfers between devices: 30.3 us -> none  [per_device(): lax.psum_scatter(lax.dot_general(smooth, data_update, (((0,), (0,)), ((),...]
    gather x2 -> x0, local copies, waits for them, and re-layouts: 19.3 us -> none  [the longest x1 9.69 us: per_device(): forward = forward_fields[data_freq].astype(jnp.float32)]
    all_gather x1 -> x0, waiting for transfers between devices: 14.4 us -> none  [per_device(): lax.all_gather(sens, 'dp', axis=0, tiled=True)]
    reduce_sum x1 -> x0, other arithmetic: 9.66 us -> none  [per_device(): jnp.sum(data_coef[:, :, None] * adjoint * forward, axis=1)]
    all_gather x1 -> x0, blocking collectives: 7.12 us -> none  [per_device(): residual_whole = lax.all_gather(residual_cols, 'dp', axis=0, tiled=True)]
    ppermute x2 -> x0, starting transfers between devices: 6.2 us -> none  [the longest x1 4.91 us: with_halo(): before = lax.ppermute(last, axis, up)]
  transfers between devices with their start and end apart: 5 -> 0, of which waited for: 3 -> 0; matrix products, arithmetic and copies ran while one was open for 2% -> 0% of each run, Pallas kernels for 0% -> 0%
where the time goes in v1:
time: 46.2 us; the launch traced here: 45.9 us
  Pallas kernels  38.4 us (83%)
  local copies, waits for them, and re-layouts  4.87 us (11%)
  other arithmetic  1.95 us (4%)
  between operations  0.71 us (2%)
    pallas_call x1, Pallas kernels, per_device(): pl.pallas_call(functools.partial(kernel, n_mp, n_dp, ka, kf), out_shape=(...  38.4 us
    unnamed x10, local copies, waits for them, and re-layouts  3.43 us
    reshape x1, local copies, waits for them, and re-layouts, per_device(): adjoint_fields.reshape(ka, cells)  1.38 us
    concatenate x1, other arithmetic, per_device(): jnp.concatenate([adjoint_fields.reshape(ka, cells), forward, forward], ax...  1.33 us

profile of v1, /device:TPU:0, one launch (start us, length us, event | category | flops | bytes accessed | tf_op | source)
XLA Modules:
  0.0 45.9 jit_solution(7562232044875286948)
XLA Ops:
  0.6 0.0 copy-start
  0.6 1.4 %reshape.12 = bf16[256,2048]{1,0:T(8,128)(2,1)S(1)} reshape(bf16[64,4,2048]{2,1,0:T(4,128)(2,1)} %param.7) | data formatting | bytes 2097152 | tf_op jit(solution)/shard_map/reshape | solution.py:275
  2.0 0.0 copy-done
  2.0 0.0 copy-start.1
  2.0 0.1 reshape.13
  2.1 0.0 copy-start.2
  2.1 0.0 copy-start.3
  2.1 1.3 %pad_maximum_fusion.af_ref = bf16[384,2048]{1,0:T(8,128)(2,1)} fusion(bf16[64,2048]{1,0:T(8,128)(2,1)S(1)} %reshape.13, bf16[256,2048]{1,0:T(8,128)(2,1)S(1)} %reshape.12), kind=kLoop, calls=%fused_computation | loop fusion | flops 4718592 | bytes 2883584 | tf_op jit(solution)/shard_map/concatenate | solution.py:275
  3.5 0.0 copy-done.1
  3.5 0.0 copy-done.2
  3.5 0.0 copy-done.3
  3.5 0.6 %select_maximum_fusion.meta_ref = f32[8,256]{1,0:T(8,128)} fusion(f32[4,192]{1,0:T(4,128)S(1)} %multiply_bitcast_fusion, f32[1,192]{1,0:T(1,128)S(1)} %bitcast.5, f32[1,192]{1,0:T(1,128)S(1)} %bitcast.4), kind=kLoop, calls=%fused_computation.1 | loop fusion | flops 22528 | bytes 12800 | tf_op jit(solution)/shard_map/concatenate | solution.py:276
  4.1 38.4 %shard_map.77 = (bf16[192,256]{1,0:T(8,128)(2,1)}, f32[512,256]{1,0:T(8,128)}) custom-call(f32[8,256]{1,0:T(8,128)} %select_maximum_fusion.meta_ref, bf16[192,256]{1,0:T(8,128)(2,1)} %r_ref.1, bf16[384,2048]{1,0:T(8,128)(2,1)} %pad_maximum_fusion.af_ref), custom_call_target="tpu_custom_call" | custom-call | tf_op jit(solution)/shard_map/pallas_call | solution.py:283
  42.5 1.5 %copy.10 = bf16[192,256]{1,0:T(8,128)(2,1)} copy(bf16[192,256]{1,0:T(8,128)(2,1)} %get-tuple-element.4) | data formatting | bytes 196608
  44.1 1.9 %copy.11 = f32[512,256]{1,0:T(8,128)} copy(f32[512,256]{1,0:T(8,128)} %get-tuple-element.5) | data formatting | bytes 1048576
  (3 shorter events, 0.0 us)
Async XLA Ops:
  0.6 1.4 %copy-start = (bf16[16,4,2048]{2,1,0:T(4,128)(2,1)S(1)}, bf16[16,4,2048]{2,1,0:T(4,128)(2,1)}, u32[]{:S(2)}) copy-start(bf16[16,4,2048]{2,1,0:T(4,128)(2,1)} %param.6) | copy-start | bytes 786436
  2.0 1.4 %copy-start.1 = (f32[192,4]{0,1:T(4,128)S(1)}, f32[192,4]{0,1:T(4,128)}, u32[]{:S(2)}) copy-start(f32[192,4]{0,1:T(4,128)} %param.10) | copy-start | bytes 9220
  2.1 1.4 %copy-start.2 = (s32[192]{0:T(256)S(1)}, s32[192]{0:T(256)}, u32[]{:S(2)}) copy-start(s32[192]{0:T(256)} %param.8) | copy-start | bytes 2308
  2.1 1.4 %copy-start.3 = (s32[192]{0:T(256)S(1)}, s32[192]{0:T(256)}, u32[]{:S(2)}) copy-start(s32[192]{0:T(256)} %param.9) | copy-start | bytes 2308

commit v2 on v1

--- a/solution.py
+++ b/solution.py
@@ -29,14 +29,14 @@
 
 def kernel(
     n_mp, n_dp, ka, kf,
-    meta_ref, r_ref, af_ref, du_ref, model_ref,
-    meta_all, r_all, win, ohr, ohf, sens, smat, smooth, smooth_t, psend, precv, q, q2, du_all,
+    rec_ref, freq_ref, coef_ref, r_ref, a_ref, f_ref, du_all, smooth_t,
+    meta, meta_all, r_all, win, ohr, ohf, sens, smat, smooth, psend, precv, q, q2,
     local_sem, halo_send, halo_recv, meta_send, meta_recv, r_send, r_recv,
     s1_send, s1_recv, s2_send, s2_recv, g_send, g_recv, d_send, d_recv,
 ):
     d, m = lax.axis_index("dp"), lax.axis_index("mp")
     rows_here, rhs = r_ref.shape
-    slab = af_ref.shape[1] // COLS
+    slab = a_ref.shape[1] // COLS
     own = slab // n_dp
     window = own + 2 * HALO
     comps = ohr.shape[0]
@@ -70,24 +70,45 @@
     def in_slab(w):
         return (slab_row(w) >= 0) & (slab_row(w) < slab)
 
+    halves = ((a_ref, slice(0, ka)), (f_ref, slice(ka, ka + kf)))
+
+    def start_all(copies):
+        for copy in copies:
+            copy.start()
+
+    def wait_all(copies):
+        for copy in copies:
+            copy.wait()
+
+    def wait_recv_all(copies):
+        for copy in copies:
+            copy.wait_recv()
+
+    def wait_send_all(copies):
+        for copy in copies:
+            copy.wait_send()
+
     def local_copy(w):
-        return pltpu.make_async_copy(
-            af_ref.at[:, grid_row(jnp.clip(slab_row(w), 0, slab - 1))],
-            win.at[:, w * COLS:(w + 1) * COLS],
-            local_sem.at[w],
-        )
+        row = grid_row(jnp.clip(slab_row(w), 0, slab - 1))
+        return [
+            pltpu.make_async_copy(ref.at[:, row], win.at[part, w * COLS:(w + 1) * COLS], local_sem.at[h, w])
+            for h, (ref, part) in enumerate(halves)
+        ]
 
     for w in range(window):
-        pl.when(in_slab(w))(local_copy(w).start)
+        pl.when(in_slab(w))(lambda w=w: start_all(local_copy(w)))
     edges = [w for w in range(window) if w < HALO or w >= own + HALO]
 
     def halo_copy(w):
         step = 1 if w < HALO else -1
-        return remote(
-            af_ref.at[:, grid_row(jnp.clip(slab_row(w) + step * slab, 0, slab - 1))],
-            win.at[:, w * COLS:(w + 1) * COLS],
-            halo_send.at[w], halo_recv.at[w], "mp", jnp.clip(m + step, 0, n_mp - 1),
-        )
+        row = grid_row(jnp.clip(slab_row(w) + step * slab, 0, slab - 1))
+        return [
+            remote(
+                ref.at[:, row], win.at[part, w * COLS:(w + 1) * COLS],
+                halo_send.at[h, w], halo_recv.at[h, w], "mp", jnp.clip(m + step, 0, n_mp - 1),
+            )
+            for h, (ref, part) in enumerate(halves)
+        ]
 
     def halo_sends(w):
         return (slab_row(w) < 0) & (m < n_mp - 1) if w < HALO else (slab_row(w) >= slab) & (m > 0)
@@ -99,27 +120,15 @@
         return (slab_row(w) < 0) & (m == 0) if w < HALO else (slab_row(w) >= slab) & (m == n_mp - 1)
 
     def meta_copy(t):
-        return remote(meta_ref, meta_all.at[d], meta_send.at[t], meta_recv.at[d], "dp", dp_peer(t))
+        return remote(meta, meta_all.at[d], meta_send.at[t], meta_recv.at[d], "dp", dp_peer(t))
 
     def r_copy(t):
         return remote(r_ref, r_all.at[block(d)], r_send.at[t], r_recv.at[d], "dp", dp_peer(t))
 
-    pl.semaphore_wait(barrier, n_dp + n_mp - 2)
-    for t in range(1, n_dp):
-        meta_copy(t).start()
-    for w in edges:
-        pl.when(halo_sends(w))(halo_copy(w).start)
-    for t in range(1, n_dp):
-        r_copy(t).start()
-
-    meta_all[d] = meta_ref[...]
-    r_all[block(d)] = r_ref[...]
-
-    def clear(w):
-        win[:, w * COLS:(w + 1) * COLS] = jnp.zeros((ka + 2 * kf, COLS), BF16)
-
-    for w in edges:
-        pl.when(beyond_grid(w))(functools.partial(clear, w))
+    meta[...] = jnp.zeros_like(meta)
+    meta[0:1, :rows_here] = rec_ref[...].astype(F32) * float(comps)
+    meta[1:2, :rows_here] = freq_ref[...].astype(F32) * float(comps)
+    meta[2:2 + comps, :rows_here] = 0.5 * coef_ref[...]
 
     at = lax.broadcasted_iota(jnp.int32, (COLS, COLS), 0)
     to = lax.broadcasted_iota(jnp.int32, (COLS, COLS), 1)
@@ -143,37 +152,72 @@
                 value = bands[gap] - missing * eye if gap == 0 else bands[gap]
             smat[w * COLS:(w + 1) * COLS, o * COLS:(o + 1) * COLS] = value.astype(BF16)
 
-    for t in range(1, n_dp):
-        source = dp_peer(t)
-        remote(meta_ref, meta_all.at[source], meta_send.at[t], meta_recv.at[source], "dp", source).wait_recv()
-    for j in range(n_dp):
+    pl.semaphore_wait(barrier, n_dp + n_mp - 2)
+    for t in range(1, n_dp):
+        meta_copy(t).start()
+    for w in edges:
+        pl.when(halo_sends(w))(lambda w=w: start_all(halo_copy(w)))
+    for t in range(1, n_dp):
+        r_copy(t).start()
+
+    meta_all[d] = meta[...]
+    r_all[block(d)] = r_ref[...]
+
+    def clear(w):
+        win[:, w * COLS:(w + 1) * COLS] = jnp.zeros((ka + 2 * kf, COLS), BF16)
+
+    for w in edges:
+        pl.when(beyond_grid(w))(functools.partial(clear, w))
+
+    def select(j):
         cols = jnp.transpose(meta_all[j])[:rows_here]
-        here = slice(j * rows_here, (j + 1) * rows_here)
+        here = block(j)
         ia = lax.broadcasted_iota(jnp.int32, (rows_here, ka), 1).astype(F32)
         jf = lax.broadcasted_iota(jnp.int32, (rows_here, kf), 1).astype(F32)
         for k in range(comps):
             ohr[k, here] = jnp.where(ia == cols[:, 0:1] + float(k), 1.0, 0.0).astype(BF16)
             weight = jnp.where(jf == cols[:, 1:2] + float(k), cols[:, 2 + k:3 + k], 0.0)
             high = weight.astype(BF16)
-            ohf[k, here, :kf] = high
-            ohf[k, here, kf:] = (weight - high.astype(F32)).astype(BF16)
+            low = (weight - high.astype(F32)).astype(BF16)
+            ohf[k, here] = jnp.concatenate([high, low], axis=1)
 
     wide = 2 if window % 2 == 0 else 1
-    tiles = sorted(range(window // wide), key=lambda i: i * wide in edges or i * wide + wide - 1 in edges)
-    for i in tiles:
+    tiles = range(window // wide)
+    edge_tiles = [i for i in tiles if any(i * wide + b in edges for b in range(wide))]
+    inner_tiles = [i for i in tiles if i not in edge_tiles]
+
+    def fields_ready(i):
         for w in range(i * wide, (i + 1) * wide):
-            pl.when(in_slab(w))(local_copy(w).wait)
+            pl.when(in_slab(w))(lambda w=w: wait_all(local_copy(w)))
             if w in edges:
-                pl.when(halo_arrives(w))(halo_copy(w).wait_recv)
+                pl.when(halo_arrives(w))(lambda w=w: wait_recv_all(halo_copy(w)))
         lanes = slice(i * wide * COLS, (i + 1) * wide * COLS)
+        win[ka + kf:, lanes] = win[ka:ka + kf, lanes]
+
+    def make_sens(i, j):
+        lanes = slice(i * wide * COLS, (i + 1) * wide * COLS)
+        here = block(j)
+        value = None
+        for k in range(comps):
+            adjoint = jnp.dot(ohr[k, here], win[:ka, lanes], preferred_element_type=F32)
+            forward = jnp.dot(ohf[k, here], win[ka:, lanes], preferred_element_type=F32)
+            value = adjoint * forward if value is None else value + adjoint * forward
+        sens[here, lanes] = value.astype(BF16)
+
+    select(d)
+    for i in inner_tiles:
+        fields_ready(i)
+        make_sens(i, d)
+    for t in range(1, n_dp):
+        source = dp_peer(t)
+        remote(meta, meta_all.at[source], meta_send.at[t], meta_recv.at[source], "dp", source).wait_recv()
+        select(source)
+        for i in inner_tiles:
+            make_sens(i, source)
+    for i in edge_tiles:
+        fields_ready(i)
         for j in range(n_dp):
-            here = slice(j * rows_here, (j + 1) * rows_here)
-            value = None
-            for k in range(comps):
-                adjoint = jnp.dot(ohr[k, here], win[:ka, lanes], preferred_element_type=F32)
-                forward = jnp.dot(ohf[k, here], win[ka:, lanes], preferred_element_type=F32)
-                value = adjoint * forward if value is None else value + adjoint * forward
-            sens[here, lanes] = value.astype(BF16)
+            make_sens(i, j)
     smooth[...] = (jnp.dot(sens[...], smat[...], preferred_element_type=F32) * 0.04).astype(BF16)
 
     for t in range(1, n_dp):
@@ -225,41 +269,58 @@
         for t in range(1, n_mp):
             g_copy(t).start()
 
-    def d_copy(t, c):
-        rows = chunk_of(d, c)
-        return remote(du_all.at[rows], du_all.at[rows], d_send.at[t, c], d_recv.at[d, c], "dp", dp_peer(t))
+    far = [2 * s for s in range(1, n_dp // 2)]
+    partner = d + 1 - 2 * lax.rem(d, 2)
+
+    def d_copy(slot, source, c, to):
+        rows = chunk_of(source, c)
+        return remote(du_all.at[rows], du_all.at[rows], d_send.at[slot, c], d_recv.at[source, c], "dp", to)
+
+    def own_copies(c):
+        return [d_copy(s, d, c, dp_peer(t)) for s, t in enumerate(far)] + [d_copy(len(far), d, c, partner)]
+
+    def relay(s, c):
+        return d_copy(len(far) + 1 + s, dp_peer(far[s]), c, partner)
 
     for c in range(chunks):
         rows = chunk_of(d, c)
         arrived = remote(du_all.at[rows], du_all.at[rows], g_send.at[0], g_recv.at[c], "mp", first + c)
         pl.when(m != first + c)(arrived.wait_recv)
-        for t in range(1, n_dp):
-            d_copy(t, c).start()
-    du_ref[...] = du_all[block(d)]
-    for t in range(1, n_dp):
-        source = dp_peer(t)
-        for c in range(chunks):
-            rows = chunk_of(source, c)
-            remote(du_all.at[rows], du_all.at[rows], d_send.at[t, c], d_recv.at[source, c], "dp", source).wait_recv()
-    model_ref[...] = jnp.dot(smooth_t[...], du_all[...], preferred_element_type=F32) * (
-        1.0 / math.sqrt(rows_here * n_dp)
-    )
+        start_all(own_copies(c))
+    for c in range(chunks):
+        for s, t in enumerate(far):
+            d_copy(0, dp_peer(t), c, dp_peer(t)).wait_recv()
+            relay(s, c).start()
+    for c in range(chunks):
+        d_copy(0, partner, c, partner).wait_recv()
+        for s, t in enumerate(far):
+            d_copy(0, lax.rem(partner + t, n_dp), c, partner).wait_recv()
 
     for w in edges:
-        pl.when(halo_sends(w))(halo_copy(w).wait_send)
+        pl.when(halo_sends(w))(lambda w=w: wait_send_all(halo_copy(w)))
     for t in range(1, n_dp):
         meta_copy(t).wait_send()
         r_copy(t).wait_send()
         p_copy(t).wait_send()
-        for c in range(chunks):
-            d_copy(t, c).wait_send()
     for c in range(chunks):
         pl.when(m != first + c)(q_copy(c).wait_send)
+        wait_send_all(own_copies(c))
+        for s in range(len(far)):
+            relay(s, c).wait_send()
 
     @pl.when(owner)
     def _():
         for t in range(1, n_mp):
             g_copy(t).wait_send()
+
+
+def finish(n_dp, smooth_t, du_all, du_ref, model_ref):
+    rows_here = du_ref.shape[0]
+    d = lax.axis_index("dp")
+    du_ref[...] = du_all[pl.ds(pl.multiple_of(d * rows_here, 16), rows_here)]
+    model_ref[...] = jnp.dot(smooth_t[...], du_all[...], preferred_element_type=F32) * (
+        1.0 / math.sqrt(rows_here * n_dp)
+    )
 
 
 def per_device(n_mp, n_dp, forward_fields, adjoint_fields, data_rec, data_freq, data_coef, residual_cols):
@@ -271,25 +332,20 @@
     own = cells // COLS // n_dp
     window = own + 2 * HALO
     chunk, chunks, first = plan(rows_here, n_mp)
-    forward = forward_fields.reshape(kf, cells)
-    af = jnp.concatenate([adjoint_fields.reshape(ka, cells), forward, forward], axis=0)
-    meta = jnp.concatenate(
-        [(data_rec * comps)[None].astype(F32), (data_freq * comps)[None].astype(F32), 0.5 * data_coef.T],
-        axis=0,
-    )
-    meta = jnp.pad(meta, ((0, 8 - meta.shape[0]), (0, -rows_here % 128)))
+    meta_shape = (8, rows_here + -rows_here % 128)
     dma = pltpu.SemaphoreType.DMA
     vmem = pl.BlockSpec(memory_space=pltpu.VMEM)
-    return pl.pallas_call(
+    du_all, smooth_t = pl.pallas_call(
         functools.partial(kernel, n_mp, n_dp, ka, kf),
         out_shape=(
-            jax.ShapeDtypeStruct((rows_here, rhs), BF16),
-            jax.ShapeDtypeStruct((own * COLS, rhs), F32),
+            jax.ShapeDtypeStruct((data, rhs), BF16),
+            jax.ShapeDtypeStruct((own * COLS, data), BF16),
         ),
-        in_specs=[vmem, vmem, pl.BlockSpec(memory_space=pl.ANY)],
+        in_specs=[vmem] * 4 + [pl.BlockSpec(memory_space=pl.ANY)] * 2,
         out_specs=(vmem, vmem),
         scratch_shapes=[
-            pltpu.VMEM((n_dp,) + meta.shape, F32),
+            pltpu.VMEM(meta_shape, F32),
+            pltpu.VMEM((n_dp,) + meta_shape, F32),
             pltpu.VMEM((data, rhs), BF16),
             pltpu.VMEM((ka + 2 * kf, window * COLS), BF16),
             pltpu.VMEM((comps, data, ka), BF16),
@@ -297,21 +353,34 @@
             pltpu.VMEM((data, window * COLS), BF16),
             pltpu.VMEM((window * COLS, own * COLS), BF16),
             pltpu.VMEM((data, own * COLS), BF16),
-            pltpu.VMEM((own * COLS, data), BF16),
             pltpu.VMEM((n_dp - 1, rows_here, rhs), BF16),
             pltpu.VMEM((n_dp, rows_here, rhs), BF16),
             pltpu.VMEM((rows_here, rhs), BF16),
             pltpu.VMEM((n_mp, chunk, rhs), BF16),
-            pltpu.VMEM((data, rhs), BF16),
-            dma((window,)), dma((window,)), dma((window,)),
+            dma((2, window)), dma((2, window)), dma((2, window)),
             dma((n_dp,)), dma((n_dp,)), dma((n_dp,)), dma((n_dp,)),
             dma((n_dp,)), dma((n_dp,)),
             dma((chunks,)), dma((n_mp,)),
             dma((n_mp,)), dma((chunks,)),
             dma((n_dp, chunks)), dma((n_dp, chunks)),
         ],
-        compiler_params=pltpu.CompilerParams(collective_id=0, has_side_effects=True, vmem_limit_bytes=60 * 1024 * 1024),
-    )(meta, residual_cols, af)
+        compiler_params=pltpu.CompilerParams(
+            collective_id=0, has_side_effects=True, vmem_limit_bytes=44 * 1024 * 1024
+        ),
+    )(
+        data_rec[None], data_freq[None], data_coef.T, residual_cols,
+        adjoint_fields.reshape(ka, cells), forward_fields.reshape(kf, cells),
+    )
+    return pl.pallas_call(
+        functools.partial(finish, n_dp),
+        out_shape=(
+            jax.ShapeDtypeStruct((rows_here, rhs), BF16),
+            jax.ShapeDtypeStruct((own * COLS, rhs), F32),
+        ),
+        in_specs=[vmem, vmem],
+        out_specs=(vmem, vmem),
+        compiler_params=pltpu.CompilerParams(vmem_limit_bytes=16 * 1024 * 1024),
+    )(smooth_t, du_all)
 
 
 def solution(mesh):

time: 46.2 us -> 38.2 us (0.83)
  Pallas kernels: 38.4 us -> 34.9 us
  local copies, waits for them, and re-layouts: 4.87 us -> 2.42 us
  other arithmetic: 1.95 us -> 0 us
    pallas_call x1, Pallas kernels: 38.4 us -> 33.7 us  [per_device(): pl.pallas_call(functools.partial(kernel, n_mp, n_dp, ka, kf), out_shape=(...]
    unnamed x10 -> x8, local copies, waits for them, and re-layouts: 3.43 us -> 0.03 us
    concatenate x2 -> x0, other arithmetic: 1.94 us -> none  [the longest x1 1.33 us: per_device(): jnp.concatenate([adjoint_fields.reshape(ka, cells), forward, forward], ax...]
    pallas_call x0 -> x1, Pallas kernels: none -> 1.17 us  [per_device(): pl.pallas_call(functools.partial(finish, n_dp), out_shape=(jax.ShapeDtype...]
    reshape x1, local copies, waits for them, and re-layouts: 0.06 us -> 1.01 us  [per_device(): forward_fields.reshape(kf, cells)]
where the time goes in v2:
time: 38.2 us; the launch traced here: 38 us
  Pallas kernels  34.9 us (91%)
  local copies, waits for them, and re-layouts  2.42 us (6%)
  between operations  0.71 us (2%)
    pallas_call x1, Pallas kernels, per_device(): pl.pallas_call(functools.partial(kernel, n_mp, n_dp, ka, kf), out_shape=(...  33.7 us
    reshape x1, local copies, waits for them, and re-layouts, per_device(): adjoint_fields.reshape(ka, cells)  1.38 us
    pallas_call x1, Pallas kernels, per_device(): pl.pallas_call(functools.partial(finish, n_dp), out_shape=(jax.ShapeDtype...  1.17 us
    reshape x1, local copies, waits for them, and re-layouts, per_device(): forward_fields.reshape(kf, cells)  1.01 us

profile of v2, /device:TPU:0, one launch (start us, length us, event | category | flops | bytes accessed | tf_op | source)
XLA Modules:
  0.0 38.0 jit_solution(10234742429947977226)
XLA Ops:
  0.6 1.0 %reshape.11.f_ref = bf16[64,2048]{1,0:T(8,128)(2,1)S(1)} reshape(bf16[16,4,2048]{2,1,0:T(4,128)(2,1)} %param.6) | data formatting | bytes 524288 | tf_op jit(solution)/shard_map/reshape | solution.py:372
  1.6 0.0 copy-start
  1.7 0.0 copy-start.1
  1.7 0.0 copy-start.2
  1.7 0.0 copy-start.3
  1.7 1.4 %reshape.10.a_ref = bf16[256,2048]{1,0:T(8,128)(2,1)S(1)} reshape(bf16[64,4,2048]{2,1,0:T(4,128)(2,1)} %param.7) | data formatting | bytes 2097152 | tf_op jit(solution)/shard_map/reshape | solution.py:372
  3.1 0.0 copy-done
  3.1 0.0 copy-done.1
  3.1 0.0 copy-done.2
  3.1 0.0 copy-done.3
  3.1 33.7 %shard_map.77 = (bf16[768,256]{1,0:T(8,128)(2,1)S(1)}, bf16[512,768]{1,0:T(8,128)(2,1)S(1)}) custom-call(s32[1,192]{1,0:T(1,128)S(1)} %bitcast.4, s32[1,192]{1,0:T(1,128)S(1)} %bitcast.5, f32[4,192]{1,0:T(4,128)S(1)} %bitcast.3, bf16[192,256]{1,0:T(8,128)(2,1)S(1)} %copy-done, bf16[256,2048]{1,0:T(8,128)(2,1)S(1)} %reshape.10.a_ref, ...), custom_call_target="tpu_custom_call" | custom-call | tf_op jit(solution)/shard_map/pallas_call | solution.py:338
  36.9 1.2 %shard_map.78 = (bf16[192,256]{1,0:T(8,128)(2,1)}, f32[512,256]{1,0:T(8,128)}) custom-call(bf16[512,768]{1,0:T(8,128)(2,1)S(1)} %get-tuple-element.4.smooth_t, bf16[768,256]{1,0:T(8,128)(2,1)S(1)} %get-tuple-element.5.du_all), custom_call_target="tpu_custom_call" | custom-call | tf_op jit(solution)/shard_map/pallas_call | solution.py:374
Async XLA Ops:
  1.6 1.4 %copy-start = (bf16[192,256]{1,0:T(8,128)(2,1)S(1)}, bf16[192,256]{1,0:T(8,128)(2,1)}, u32[]{:S(2)}) copy-start(bf16[192,256]{1,0:T(8,128)(2,1)} %r_ref.1) | copy-start | bytes 294916
  1.7 1.4 %copy-start.1 = (f32[192,4]{0,1:T(4,128)S(1)}, f32[192,4]{0,1:T(4,128)}, u32[]{:S(2)}) copy-start(f32[192,4]{0,1:T(4,128)} %param.10) | copy-start | bytes 9220
  1.7 1.4 %copy-start.2 = (s32[192]{0:T(256)S(1)}, s32[192]{0:T(256)}, u32[]{:S(2)}) copy-start(s32[192]{0:T(256)} %param.8) | copy-start | bytes 2308
  1.7 1.4 %copy-start.3 = (s32[192]{0:T(256)S(1)}, s32[192]{0:T(256)}, u32[]{:S(2)}) copy-start(s32[192]{0:T(256)} %param.9) | copy-start | bytes 2308

commit v3 on v2

--- a/solution.py
+++ b/solution.py
@@ -152,22 +152,7 @@
                 value = bands[gap] - missing * eye if gap == 0 else bands[gap]
             smat[w * COLS:(w + 1) * COLS, o * COLS:(o + 1) * COLS] = value.astype(BF16)
 
-    pl.semaphore_wait(barrier, n_dp + n_mp - 2)
-    for t in range(1, n_dp):
-        meta_copy(t).start()
-    for w in edges:
-        pl.when(halo_sends(w))(lambda w=w: start_all(halo_copy(w)))
-    for t in range(1, n_dp):
-        r_copy(t).start()
-
     meta_all[d] = meta[...]
-    r_all[block(d)] = r_ref[...]
-
-    def clear(w):
-        win[:, w * COLS:(w + 1) * COLS] = jnp.zeros((ka + 2 * kf, COLS), BF16)
-
-    for w in edges:
-        pl.when(beyond_grid(w))(functools.partial(clear, w))
 
     def select(j):
         cols = jnp.transpose(meta_all[j])[:rows_here]
@@ -181,6 +166,23 @@
             low = (weight - high.astype(F32)).astype(BF16)
             ohf[k, here] = jnp.concatenate([high, low], axis=1)
 
+    select(d)
+    pl.semaphore_wait(barrier, n_dp + n_mp - 2)
+    for t in range(1, n_dp):
+        meta_copy(t).start()
+    for w in edges:
+        pl.when(halo_sends(w))(lambda w=w: start_all(halo_copy(w)))
+    for t in range(1, n_dp):
+        r_copy(t).start()
+
+    r_all[block(d)] = r_ref[...]
+
+    def clear(w):
+        win[:, w * COLS:(w + 1) * COLS] = jnp.zeros((ka + 2 * kf, COLS), BF16)
+
+    for w in edges:
+        pl.when(beyond_grid(w))(functools.partial(clear, w))
+
     wide = 2 if window % 2 == 0 else 1
     tiles = range(window // wide)
     edge_tiles = [i for i in tiles if any(i * wide + b in edges for b in range(wide))]
@@ -204,7 +206,6 @@
             value = adjoint * forward if value is None else value + adjoint * forward
         sens[here, lanes] = value.astype(BF16)
 
-    select(d)
     for i in inner_tiles:
         fields_ready(i)
         make_sens(i, d)
@@ -333,6 +334,7 @@
     window = own + 2 * HALO
     chunk, chunks, first = plan(rows_here, n_mp)
     meta_shape = (8, rows_here + -rows_here % 128)
+    adjoint, forward = lax.optimization_barrier((adjoint_fields.reshape(ka, cells), forward_fields))
     dma = pltpu.SemaphoreType.DMA
     vmem = pl.BlockSpec(memory_space=pltpu.VMEM)
     du_all, smooth_t = pl.pallas_call(
@@ -369,7 +371,7 @@
         ),
     )(
         data_rec[None], data_freq[None], data_coef.T, residual_cols,
-        adjoint_fields.reshape(ka, cells), forward_fields.reshape(kf, cells),
+        adjoint, forward.reshape(kf, cells),
     )
     return pl.pallas_call(
         functools.partial(finish, n_dp),

time: 38.2 us -> 38.3 us (level)
    reshape x1, local copies, waits for them, and re-layouts: 1.01 us -> 0.06 us  [per_device(): forward.reshape(kf, cells)]
    unnamed x8 -> x10, local copies, waits for them, and re-layouts: 0.03 us -> 0.81 us
where the time goes in v3:
time: 38.3 us; the launch traced here: 38.1 us
  Pallas kernels  35.2 us (92%)
  local copies, waits for them, and re-layouts  2.25 us (6%)
  between operations  0.7 us (2%)
    pallas_call x1, Pallas kernels, per_device(): pl.pallas_call(functools.partial(kernel, n_mp, n_dp, ka, kf), out_shape=(...  34 us
    reshape x1, local copies, waits for them, and re-layouts, per_device(): adjoint_fields.reshape(ka, cells)  1.38 us
    pallas_call x1, Pallas kernels, per_device(): pl.pallas_call(functools.partial(finish, n_dp), out_shape=(jax.ShapeDtype...  1.18 us
    unnamed x10, local copies, waits for them, and re-layouts  0.81 us

profile of v3, /device:TPU:0, one launch (start us, length us, event | category | flops | bytes accessed | tf_op | source)
XLA Modules:
  0.0 38.1 jit_solution(12658262408849967847)
XLA Ops:
  0.6 0.0 copy-start.4
  0.6 1.4 %reshape.10.a_ref = bf16[256,2048]{1,0:T(8,128)(2,1)S(1)} reshape(bf16[64,4,2048]{2,1,0:T(4,128)(2,1)} %param.7) | data formatting | bytes 2097152 | tf_op jit(solution)/shard_map/reshape | solution.py:337
  2.0 0.0 copy-done.4
  2.0 0.0 copy-start
  2.0 0.0 copy-start.1
  2.1 0.0 copy-start.2
  2.1 0.0 copy-start.3
  2.1 0.1 reshape.11.f_ref
  2.2 0.8 %copy-done = bf16[192,256]{1,0:T(8,128)(2,1)S(1)} copy-done((bf16[192,256]{1,0:T(8,128)(2,1)S(1)}, bf16[192,256]{1,0:T(8,128)(2,1)}, u32[]{:S(2)}) %copy-start) | copy-done | bytes 98328
  2.9 0.0 copy-done.1
  2.9 0.0 copy-done.2
  2.9 0.0 copy-done.3
  2.9 34.0 %shard_map.77 = (bf16[768,256]{1,0:T(8,128)(2,1)S(1)}, bf16[512,768]{1,0:T(8,128)(2,1)S(1)}) custom-call(s32[1,192]{1,0:T(1,128)S(1)} %bitcast.4, s32[1,192]{1,0:T(1,128)S(1)} %bitcast.5, f32[4,192]{1,0:T(4,128)S(1)} %bitcast.3, bf16[192,256]{1,0:T(8,128)(2,1)S(1)} %copy-done, bf16[256,2048]{1,0:T(8,128)(2,1)S(1)} %reshape.10.a_ref, ...), custom_call_target="tpu_custom_call" | custom-call | tf_op jit(solution)/shard_map/pallas_call | solution.py:340
  37.0 1.2 %shard_map.78 = (bf16[192,256]{1,0:T(8,128)(2,1)}, f32[512,256]{1,0:T(8,128)}) custom-call(bf16[512,768]{1,0:T(8,128)(2,1)S(1)} %get-tuple-element.8.smooth_t, bf16[768,256]{1,0:T(8,128)(2,1)S(1)} %get-tuple-element.9.du_all), custom_call_target="tpu_custom_call" | custom-call | tf_op jit(solution)/shard_map/pallas_call | solution.py:376
Async XLA Ops:
  0.6 1.4 %copy-start.4 = (bf16[16,4,2048]{2,1,0:T(4,128)(2,1)S(1)}, bf16[16,4,2048]{2,1,0:T(4,128)(2,1)}, u32[]{:S(2)}) copy-start(bf16[16,4,2048]{2,1,0:T(4,128)(2,1)} %param.6) | copy-start | bytes 786436
  2.0 0.9 %copy-start = (bf16[192,256]{1,0:T(8,128)(2,1)S(1)}, bf16[192,256]{1,0:T(8,128)(2,1)}, u32[]{:S(2)}) copy-start(bf16[192,256]{1,0:T(8,128)(2,1)} %r_ref.1) | copy-start | bytes 294916
  2.0 0.9 %copy-start.1 = (f32[192,4]{0,1:T(4,128)S(1)}, f32[192,4]{0,1:T(4,128)}, u32[]{:S(2)}) copy-start(f32[192,4]{0,1:T(4,128)} %param.10) | copy-start | bytes 9220
  2.1 0.9 %copy-start.2 = (s32[192]{0:T(256)S(1)}, s32[192]{0:T(256)}, u32[]{:S(2)}) copy-start(s32[192]{0:T(256)} %param.8) | copy-start | bytes 2308
  2.1 0.9 %copy-start.3 = (s32[192]{0:T(256)S(1)}, s32[192]{0:T(256)}, u32[]{:S(2)}) copy-start(s32[192]{0:T(256)} %param.9) | copy-start | bytes 2308
